TPU v7x, 32 devices: a whole 2x2x4 slice. The times are simulated.
32 devices in a mesh: dp: 4 (over z), rep: 2 (over y), grp: 4 (over x, core).
Axes of the slice: x: 2, y: 2, z: 4, core: 2. Of those that a mesh axis runs over, the one named last changes fastest.
Arguments:
- grad_parts: float32 [8, 8, 192, 2048], P(('rep', 'grp'), None, 'dp'), may hold values from -6 to 6
- momentum: float32 [8, 192, 2048], P(None, 'dp', ('rep', 'grp')), may hold values from -24 to 24
- layer_live: int32 [8], replicated, may hold values from 0 to 1, as said below
Outputs:
- new_momentum: float32 [8, 192, 2048], P(None, 'dp', ('rep', 'grp'))
- orth_update: bfloat16 [8, 192, 2048], P(None, 'dp', ('rep', 'grp'))
Inputs may be any that keep to these rules, and one draw needn't show every extreme that they name: `layer_live`: at least one matrix is live in every draw.
All inputs are finite; a program needn't handle non-finite values.
Results may differ from a plain program's by a relative error of at most 0.028.
Values may be sent and summed in bfloat16 or wider, within the bound.
A program may use at most 64 MiB of HBM per device.

v0:
```python
import math

import jax
import jax.numpy as jnp
from jax import lax
from jax.sharding import PartitionSpec as P

ITERS = 5


decay_rate = 0.95
first_coef = 3.4445
second_coef = -4.775
third_coef = 2.0315
norm_eps = 1e-07


def newton_schulz(source):
    source_f32 = source.astype(jnp.float32)
    frob_norm = jnp.sqrt(jnp.sum(source_f32 * source_f32))
    current = (source_f32 / (frob_norm + norm_eps)).astype(jnp.bfloat16)
    next_iterate = source_f32
    for iteration in range(ITERS):
        gram_matrix = lax.dot_general(
            current, current, (((1,), (1,)), ((), ())), preferred_element_type=jnp.float32
        ).astype(jnp.bfloat16)
        squared = jnp.dot(gram_matrix, gram_matrix, preferred_element_type=jnp.float32)
        polynomial = (second_coef * gram_matrix.astype(jnp.float32) + third_coef * squared).astype(
            jnp.bfloat16
        )
        next_iterate = first_coef * current.astype(jnp.float32) + jnp.dot(
            polynomial, current, preferred_element_type=jnp.float32
        )
        if iteration + 1 < ITERS:
            current = next_iterate.astype(jnp.bfloat16)
    return (next_iterate * math.sqrt(source.shape[1])).astype(jnp.bfloat16)


def zero_result(matrix):
    return jnp.zeros_like(matrix)


def guarded(matrix):
    return lax.cond(jnp.any(matrix != 0), newton_schulz, zero_result, matrix)


def per_device(grad_parts, momentum, layer_live):
    width = momentum.shape[2]
    col_start = lax.axis_index(("rep", "grp")) * width
    active = (layer_live > 0)[:, None, None]
    summed_share = lax.psum_scatter(grad_parts[0], ("rep", "grp"), scatter_dimension=2, tiled=True)
    fresh_momentum = jnp.where(active, decay_rate * momentum + summed_share, momentum)
    sources = lax.all_gather(
        fresh_momentum.astype(jnp.bfloat16), ("rep", "grp"), axis=2, tiled=True
    )
    owners = lax.axis_size("dp")
    matrices = layer_live.shape[0]
    per_owner = matrices // owners
    piece_rows = sources.shape[1]
    col_count = sources.shape[2]
    matrix_ids = jnp.arange(matrices, dtype=jnp.int32)
    live_flag = (layer_live > 0).astype(jnp.int32)
    slot_pos = matrix_ids % per_owner * owners + matrix_ids // per_owner
    slot_ids = jnp.arange(matrices, dtype=jnp.int32)
    placing = slot_pos[None, :] == slot_ids[:, None]
    holder = jnp.sum(jnp.where(placing, matrix_ids[None, :], 0), axis=1)
    filled = jnp.sum(placing.astype(jnp.int32) * live_flag[None, :], axis=1)
    picked_rows = jnp.take(sources, holder, axis=0)
    outgoing = jnp.where(filled[:, None, None] > 0, picked_rows, jnp.zeros_like(picked_rows))
    outgoing = outgoing.reshape(per_owner, owners, piece_rows, col_count)
    blocks = lax.all_to_all(outgoing, "dp", split_axis=1, concat_axis=1, tiled=True)
    item_count = blocks.shape[0]
    stacked = blocks.reshape(item_count, owners * piece_rows, col_count)
    results = lax.map(guarded, stacked)
    results = results.reshape(item_count, owners, piece_rows, col_count)
    returned = lax.all_to_all(results, "dp", split_axis=1, concat_axis=1, tiled=True)
    returned = returned.reshape(matrices, piece_rows, col_count)
    own_cols = lax.dynamic_slice_in_dim(returned, col_start, width, 2)
    gathered = jnp.take(own_cols, jnp.maximum(slot_pos, 0), axis=0)
    orth_update = jnp.where(active, gathered, jnp.zeros_like(gathered))
    return (fresh_momentum, orth_update)


def solution(mesh):
    placed = (P(("rep", "grp"), None, "dp", None), P(None, "dp", ("rep", "grp")), P())
    return jax.shard_map(
        per_device,
        mesh=mesh,
        in_specs=placed,
        out_specs=(P(None, "dp", ("rep", "grp")), P(None, "dp", ("rep", "grp"))),
        check_vma=False,
    )
```

profile of v0, /device:TPU:0, one launch (start us, length us, event | category | flops | bytes accessed | tf_op | source)
XLA Modules:
  0.0 203.2 jit_solution(3120309058934634420)
XLA Ops:
  7.2 0.0 reduce-scatter.2.cloned.1.call-start
  7.2 0.0 copy-start.3
  7.2 0.0 copy-start.2
  7.2 0.7 reduce-scatter.2.cloned.1.call-update
  7.9 0.0 all-gather.2.cloned.1.call-start
  7.9 0.0 copy-done.3
  8.0 52.2 %reduce-scatter.2.cloned.1.call-done = f32[8,48,256]{2,1,0:T(8,128)} async-done(((f32[8,48,2048]{2,1,0:T(8,128)}), f32[8,48,256]{2,1,0:T(8,128)}) %reduce-scatter.2.cloned.1.call-update) | async-done | bytes 393232 | tf_op jit(solution)/shard_map/reduce_scatter | solution.py:51
  60.1 0.0 copy-done.2
  60.2 1.9 fusion.60
  62.1 0.0 all-gather.2.cloned.1.call-update
  62.1 0.1 select_reduce_fusion.1
  62.2 0.1 reduce_sum.33
  62.3 0.1 copy.16
  62.5 0.1 gt.17
  62.5 0.1 copy.15
  62.7 25.8 %all-gather.2.cloned.1.call-done = bf16[8,48,2048]{2,1,0:T(8,128)(2,1)} async-done(((bf16[8,48,256]{2,1,0:T(8,128)(2,1)}), bf16[8,48,2048]{2,1,0:T(8,128)(2,1)}) %all-gather.2.cloned.1.call-update) | async-done | bytes 1572880 | tf_op jit(solution)/shard_map/all_gather | solution.py:53
  88.4 2.1 %gather_fusion = bf16[8,48,2048]{2,1,0:T(8,128)(2,1)S(1)} fusion(bf16[8,48,2048]{2,1,0:T(8,128)(2,1)} %all-gather.2.cloned.1.call-done, s32[1024]{0:T(1024)S(1)} %pad_clamp_fusion.1), kind=kCustom, calls=%fused_computation | custom fusion | bytes 3145760 | tf_op jit(solution)/shard_map/jit(_take)/gather | solution.py:68
  90.5 1.4 fusion.51
  91.9 4.6 %all-to-all-start = ((bf16[2,4,48,2048]{3,2,0,1:T(8,128)(2,1)}), bf16[2,4,48,2048]{3,2,0,1:T(8,128)(2,1)S(1)}, u32[]{:S(2)}, u32[]{:S(2)}) async-start(bf16[2,4,48,2048]{3,2,0,1:T(8,128)(2,1)} %fusion.51), calls=%async_computation.1 | async-start | bytes 3145728 | tf_op jit(solution)/shard_map/all_to_all | solution.py:71
  96.5 37.4 %all-to-all-done = bf16[2,4,48,2048]{3,2,0,1:T(8,128)(2,1)S(1)} async-done(((bf16[2,4,48,2048]{3,2,0,1:T(8,128)(2,1)}), bf16[2,4,48,2048]{3,2,0,1:T(8,128)(2,1)S(1)}, u32[]{:S(2)}, u32[]{:S(2)}) %all-to-all-start) | async-done | bytes 1572896 | tf_op jit(solution)/shard_map/all_to_all | solution.py:71
  133.9 0.2 copy.18
  134.0 12.9 %while.10 = (s32[]{:T(128)}, bf16[2,192,2048]{2,1,0:T(8,128)(2,1)}, bf16[2,192,2048]{2,1,0:T(8,128)(2,1)S(1)}, s32[]{:T(128)}) while((s32[]{:T(128)}, bf16[2,192,2048]{2,1,0:T(8,128)(2,1)}, bf16[2,192,2048]{2,1,0:T(8,128)(2,1)S(1)}, s32[]{:T(128)}) %tuple.48), condition=%wide.region_8.9_spmd, body=%wide.region_3.8_spmd.sunk | while | flops 1595596800 | bytes 29049504 | solution.py:74
  134.0 0.0 copy-start
  134.1 1.0 compare_reduce_fusion.2
  135.6 0.0 copy-done
  135.6 6.2 %conditional.2 = (bf16[1,192,2048]{2,1,0:T(8,128)(2,1)S(1)}) conditional(s32[]{:T(128)} %convert_element_type.165, () %tuple.38, bf16[192,2048]{1,0:T(8,128)(2,1)S(1)} %get-tuple-element.62), branch_computations={%region_5.5_spmd, %region_6.7_spmd} | conditional | flops 1594810368 | bytes 13320232 | solution.py:44
  135.6 1.0 fusion.7
  137.2 0.4 convolution_convert_fusion.4
  137.7 0.5 fusion.2
  138.2 0.4 convolution_convert_fusion.3
  138.6 0.5 fusion.3
  139.1 0.4 convolution_convert_fusion.2
  139.5 0.5 fusion.4
  140.0 0.4 convolution_convert_fusion.1
  140.4 0.5 fusion.5
  140.9 0.4 convolution_convert_fusion
  141.3 0.5 fusion.6
  141.9 0.0 copy-start.1
  141.9 1.0 constant_dynamic-update-slice_fusion.2
  142.8 0.7 copy-done.1
  143.6 0.0 copy-start
  143.6 1.0 compare_reduce_fusion.2
  145.1 0.0 copy-done
  145.1 0.1 conditional.2
  145.1 0.1 broadcast_in_dim.63
  145.2 0.0 copy-start.1
  145.2 0.9 constant_dynamic-update-slice_fusion.2
  146.2 0.7 copy-done.1
  146.9 2.7 %copy.19 = bf16[2,4,48,2048]{3,2,0,1:T(8,128)(2,1)} copy(bf16[2,4,48,2048]{3,2,1,0:T(8,128)(2,1)} %bitcast.42) | data formatting | bytes 3145728 | tf_op jit(solution)/shard_map/reshape | solution.py:75
  149.7 8.9 %all-to-all-start.1 = ((bf16[2,4,48,2048]{3,2,0,1:T(8,128)(2,1)}), bf16[2,4,48,2048]{3,2,0,1:T(8,128)(2,1)S(1)}, u32[]{:S(2)}, u32[]{:S(2)}) async-start(bf16[2,4,48,2048]{3,2,0,1:T(8,128)(2,1)} %copy.19), calls=%async_computation.2 | async-start | bytes 3145728 | tf_op jit(solution)/shard_map/all_to_all | solution.py:76
  158.6 36.2 %all-to-all-done.1 = bf16[2,4,48,2048]{3,2,0,1:T(8,128)(2,1)S(1)} async-done(((bf16[2,4,48,2048]{3,2,0,1:T(8,128)(2,1)}), bf16[2,4,48,2048]{3,2,0,1:T(8,128)(2,1)S(1)}, u32[]{:S(2)}, u32[]{:S(2)}) %all-to-all-start.1) | async-done | bytes 1572896 | tf_op jit(solution)/shard_map/all_to_all | solution.py:76
  194.8 0.2 copy.20
  195.0 0.6 gather_fusion.1
  195.6 0.8 select_select_fusion
  (10 shorter events, 0.1 us)
Async XLA Ops:
  7.2 53.0 %reduce-scatter.2.cloned.1.call-start = ((), (), s32[]{:S(2)}) async-start(), calls=%async_computation.3 | async-start | bytes 3538944 | tf_op jit(solution)/shard_map/reduce_scatter | solution.py:51
  7.2 0.7 copy-start.3
  7.2 52.9 %copy-start.2 = (f32[8,48,256]{2,1,0:T(8,128)S(1)}, f32[8,48,256]{2,1,0:T(8,128)}, u32[]{:S(2)}) copy-start(f32[8,48,256]{2,1,0:T(8,128)} %param.8) | copy-start | bytes 1179652
  7.9 80.5 %all-gather.2.cloned.1.call-start = ((), (), s32[]{:S(2)}) async-start(), calls=%async_computation.4 | async-start | bytes 1769472 | tf_op jit(solution)/shard_map/all_gather | solution.py:53
  91.9 42.0 %all-to-all-start = ((bf16[2,4,48,2048]{3,2,0,1:T(8,128)(2,1)}), bf16[2,4,48,2048]{3,2,0,1:T(8,128)(2,1)S(1)}, u32[]{:S(2)}, u32[]{:S(2)}) async-start(bf16[2,4,48,2048]{3,2,0,1:T(8,128)(2,1)} %fusion.51), calls=%async_computation.1 | async-start | bytes 3145728 | tf_op jit(solution)/shard_map/all_to_all | solution.py:71
  134.0 1.6 copy-start
  141.9 1.7 copy-start.1
  143.6 1.6 copy-start
  145.2 1.7 copy-start.1
  149.7 45.1 %all-to-all-start.1 = ((bf16[2,4,48,2048]{3,2,0,1:T(8,128)(2,1)}), bf16[2,4,48,2048]{3,2,0,1:T(8,128)(2,1)S(1)}, u32[]{:S(2)}, u32[]{:S(2)}) async-start(bf16[2,4,48,2048]{3,2,0,1:T(8,128)(2,1)} %copy.19), calls=%async_computation.2 | async-start | bytes 3145728 | tf_op jit(solution)/shard_map/all_to_all | solution.py:76
Sparse Core Ops, SparseCore 0:
  11.3 48.7 reduce-scatter.1
  62.6 25.7 all-gather.1
where the time goes:
time: 202 us; the launch traced here: 203 us
  waiting for transfers between devices  152 us (75%)
  between operations  14.1 us (7%)
  starting transfers between devices  13.6 us (7%)
  local copies, waits for them, and re-layouts  9.57 us (5%)
  other arithmetic  7.27 us (4%)
  matrix products  4.55 us (2%)
    reduce_scatter x1, waiting for transfers between devices, per_device(): lax.psum_scatter(grad_parts[0], ('rep', 'grp'), scatter_dimension=2, tile...  52.2 us
    all_to_all x1, waiting for transfers between devices, per_device(): lax.all_to_all(outgoing, 'dp', split_axis=1, concat_axis=1, tiled=True)  37.4 us
    all_to_all x1, waiting for transfers between devices, per_device(): lax.all_to_all(results, 'dp', split_axis=1, concat_axis=1, tiled=True)  36.2 us
    all_gather x1, waiting for transfers between devices, per_device(): lax.all_gather(fresh_momentum.astype(jnp.bfloat16), ('rep', 'grp'), axis=...  25.8 us
    all_to_all x1, starting transfers between devices, per_device(): lax.all_to_all(results, 'dp', split_axis=1, concat_axis=1, tiled=True)  8.88 us
    all_to_all x1, starting transfers between devices, per_device(): lax.all_to_all(outgoing, 'dp', split_axis=1, concat_axis=1, tiled=True)  4.6 us
  transfers between devices with their start and end apart: 4, of which 4 were waited for; matrix products, arithmetic and copies ran while one was open for 0% of the time, Pallas kernels for 0%

commit v1 on v0

--- a/solution.py
+++ b/solution.py
@@ -1,8 +1,11 @@
+import functools
 import math
 
 import jax
 import jax.numpy as jnp
 from jax import lax
+from jax.experimental import pallas as pl
+from jax.experimental.pallas import tpu as pltpu
 from jax.sharding import PartitionSpec as P
 
 ITERS = 5
@@ -81,10 +84,257 @@
     return (fresh_momentum, orth_update)
 
 
+MESH = pl.DeviceIdType.MESH
+
+
+def f32_dot(left, right):
+    return jnp.dot(
+        left.astype(jnp.bfloat16), right.astype(jnp.bfloat16), preferred_element_type=jnp.float32
+    )
+
+
+def orthogonalizer(gram):
+    rows = gram.shape[0]
+    row_ids = lax.broadcasted_iota(jnp.int32, (rows, rows), 0)
+    col_ids = lax.broadcasted_iota(jnp.int32, (rows, rows), 1)
+    on_diag = row_ids == col_ids
+    diag = jnp.where(on_diag, gram, 0.0)
+    squares = jnp.sum(jnp.sum(diag, axis=1, keepdims=True), axis=0, keepdims=True)
+    inverse = 1.0 / (jnp.sqrt(squares) + norm_eps)
+    current = gram * inverse * inverse
+    product = None
+    for iteration in range(ITERS):
+        squared = f32_dot(current, current)
+        higher = second_coef * current + third_coef * squared
+        if product is None:
+            product = jnp.where(on_diag, first_coef, 0.0) + higher
+        else:
+            product = first_coef * product + f32_dot(higher, product)
+        if iteration + 1 < ITERS:
+            half = first_coef * current + f32_dot(higher, current)
+            current = first_coef * half + f32_dot(higher, half)
+    return product * inverse
+
+
+def step_kernel(
+    sizes, grad_ref, mom_ref, live_ref, new_ref, orth_ref,
+    gbuf, sbuf, rbuf, zsend, xbuf, gsend, grecv, gsum, gfull, osend, orecv,
+    lsem, ssem, rsem, zssem, zrsem, gssem, grsem, assem, arsem, ossem, orsem, csem,
+):
+    group, owners, per_group, n, rows, width = sizes
+    per = n // owners
+    full = owners * rows
+    share = per * full // group
+    me_d = lax.axis_index("dp")
+    me = lax.axis_index("rep") * per_group + lax.axis_index("grp")
+
+    def peer_index(k):
+        return lax.rem(me + k, group)
+
+    def peer_id(k):
+        peer = peer_index(k)
+        return {"rep": peer // per_group, "grp": lax.rem(peer, per_group)}
+
+    def owner_index(k):
+        return lax.rem(me_d + k, owners)
+
+    loads = []
+    for k in list(range(1, group)) + [0]:
+        start = pl.multiple_of(peer_index(k) * width, width)
+        load = pltpu.make_async_copy(
+            grad_ref.at[0, :, :, pl.ds(start, width)], gbuf.at[k], lsem.at[k]
+        )
+        load.start()
+        loads.append(load)
+    barrier = pltpu.get_barrier_semaphore()
+    for k in range(1, group):
+        pl.semaphore_signal(barrier, inc=1, device_id=peer_id(k), device_id_type=MESH)
+    for k in range(1, owners):
+        pl.semaphore_signal(barrier, inc=1, device_id={"dp": owner_index(k)}, device_id_type=MESH)
+    pl.semaphore_wait(barrier, group + owners - 2)
+
+    sends = []
+    for k in range(1, group):
+        loads[k - 1].wait()
+        sbuf[k - 1] = gbuf[k].astype(jnp.bfloat16)
+        copy = pltpu.make_async_remote_copy(
+            src_ref=sbuf.at[k - 1], dst_ref=rbuf.at[k - 1],
+            send_sem=ssem.at[k - 1], recv_sem=rsem.at[k - 1],
+            device_id=peer_id(k), device_id_type=MESH,
+        )
+        copy.start()
+        sends.append(copy)
+    loads[group - 1].wait()
+    for copy in sends:
+        copy.wait_recv()
+    for i in range(n):
+        total = gbuf[0, i]
+        for k in range(1, group):
+            total = total + rbuf[k - 1, i].astype(jnp.float32)
+        old = mom_ref[i]
+        fresh = jnp.where(live_ref[i] > 0, decay_rate * old + total, old)
+        new_ref[i] = fresh
+        zsend[i] = fresh.astype(jnp.bfloat16)
+
+    my_rows = pl.ds(pl.multiple_of(me_d * rows, rows), rows)
+    own = pltpu.make_async_copy(
+        zsend.at[pl.ds(me_d * per, per)], xbuf.at[:, my_rows, :], csem.at[0]
+    )
+    own.start()
+    zcopies = []
+    for k in range(1, owners):
+        copy = pltpu.make_async_remote_copy(
+            src_ref=zsend.at[pl.ds(owner_index(k) * per, per)], dst_ref=xbuf.at[:, my_rows, :],
+            send_sem=zssem.at[k - 1], recv_sem=zrsem.at[k - 1],
+            device_id={"dp": owner_index(k)}, device_id_type=MESH,
+        )
+        copy.start()
+        zcopies.append(copy)
+    own.wait()
+    for copy in zcopies:
+        copy.wait_recv()
+
+    for m in range(per):
+        block = xbuf[m]
+        gram = lax.dot_general(
+            block, block, (((1,), (1,)), ((), ())), preferred_element_type=jnp.float32
+        )
+        gsend[m * full : (m + 1) * full] = gram.astype(jnp.bfloat16)
+    gcopies = []
+    for k in range(1, group):
+        start = pl.multiple_of(peer_index(k) * share, share)
+        copy = pltpu.make_async_remote_copy(
+            src_ref=gsend.at[pl.ds(start, share)], dst_ref=grecv.at[k - 1],
+            send_sem=gssem.at[k - 1], recv_sem=grsem.at[k - 1],
+            device_id=peer_id(k), device_id_type=MESH,
+        )
+        copy.start()
+        gcopies.append(copy)
+    my_share = pl.ds(pl.multiple_of(me * share, share), share)
+    total = gsend[my_share].astype(jnp.float32)
+    for k in range(1, group):
+        gcopies[k - 1].wait_recv()
+        total = total + grecv[k - 1].astype(jnp.float32)
+    gsum[...] = total.astype(jnp.bfloat16)
+    acopies = []
+    for k in range(1, group):
+        copy = pltpu.make_async_remote_copy(
+            src_ref=gsum, dst_ref=gfull.at[my_share],
+            send_sem=assem.at[k - 1], recv_sem=arsem.at[k - 1],
+            device_id=peer_id(k), device_id_type=MESH,
+        )
+        copy.start()
+        acopies.append(copy)
+    gfull[my_share] = gsum[...]
+    for copy in acopies:
+        copy.wait_recv()
+
+    scale = math.sqrt(width * group)
+    factors = [
+        (orthogonalizer(gfull[m * full : (m + 1) * full].astype(jnp.float32)) * scale)
+        for m in range(per)
+    ]
+    for m in range(per):
+        osend[m] = f32_dot(factors[m], xbuf[m]).astype(jnp.bfloat16)
+    own = pltpu.make_async_copy(
+        osend.at[:, my_rows, :], orecv.at[pl.ds(me_d * per, per)], csem.at[1]
+    )
+    own.start()
+    ocopies = []
+    for k in range(1, owners):
+        their_rows = pl.ds(pl.multiple_of(owner_index(k) * rows, rows), rows)
+        copy = pltpu.make_async_remote_copy(
+            src_ref=osend.at[:, their_rows, :], dst_ref=orecv.at[pl.ds(me_d * per, per)],
+            send_sem=ossem.at[k - 1], recv_sem=orsem.at[k - 1],
+            device_id={"dp": owner_index(k)}, device_id_type=MESH,
+        )
+        copy.start()
+        ocopies.append(copy)
+    for copies in (sends, zcopies, gcopies, acopies):
+        for copy in copies:
+            copy.wait_send()
+    own.wait()
+    for copy in ocopies:
+        copy.wait_recv()
+    for i in range(n):
+        part = orecv[i]
+        orth_ref[i] = jnp.where(live_ref[i] > 0, part.astype(jnp.float32), 0.0).astype(jnp.bfloat16)
+    for copy in ocopies:
+        copy.wait_send()
+
+
+def fused_step(mesh, grad_parts, momentum, layer_live):
+    n, rows, width = momentum.shape
+    owners, per_group = mesh.shape["dp"], mesh.shape["grp"]
+    group = mesh.shape["rep"] * per_group
+    per = n // owners
+    full = owners * rows
+    share = per * full // group
+    live = jnp.broadcast_to(layer_live.astype(jnp.float32)[:, None, None], (n, 1, width))
+    bf16, f32 = jnp.bfloat16, jnp.float32
+    dma = pltpu.SemaphoreType.DMA
+    vmem = pl.BlockSpec(memory_space=pltpu.VMEM)
+    return pl.pallas_call(
+        functools.partial(step_kernel, (group, owners, per_group, n, rows, width)),
+        out_shape=(
+            jax.ShapeDtypeStruct((n, rows, width), f32),
+            jax.ShapeDtypeStruct((n, rows, width), bf16),
+        ),
+        in_specs=[pl.BlockSpec(memory_space=pl.ANY), vmem, vmem],
+        out_specs=(vmem, vmem),
+        scratch_shapes=[
+            pltpu.VMEM((group, n, rows, width), f32),
+            pltpu.VMEM((group - 1, n, rows, width), bf16),
+            pltpu.VMEM((group - 1, n, rows, width), bf16),
+            pltpu.VMEM((n, rows, width), bf16),
+            pltpu.VMEM((per, full, width), bf16),
+            pltpu.VMEM((per * full, full), bf16),
+            pltpu.VMEM((group - 1, share, full), bf16),
+            pltpu.VMEM((share, full), bf16),
+            pltpu.VMEM((per * full, full), bf16),
+            pltpu.VMEM((per, full, width), bf16),
+            pltpu.VMEM((n, rows, width), bf16),
+            dma((group,)),
+            dma((group - 1,)),
+            dma((group - 1,)),
+            dma((owners - 1,)),
+            dma((owners - 1,)),
+            dma((group - 1,)),
+            dma((group - 1,)),
+            dma((group - 1,)),
+            dma((group - 1,)),
+            dma((owners - 1,)),
+            dma((owners - 1,)),
+            dma((2,)),
+        ],
+        compiler_params=pltpu.CompilerParams(
+            collective_id=0, has_side_effects=True, vmem_limit_bytes=48 * 1024 * 1024
+        ),
+    )(grad_parts, momentum, live)
+
+
+def per_device_step(mesh, grad_parts, momentum, layer_live):
+    n, rows, width = momentum.shape
+    owners = mesh.shape["dp"]
+    group = mesh.shape["rep"] * mesh.shape["grp"]
+    fits = (
+        width % 128 == 0
+        and rows % 16 == 0
+        and n % owners == 0
+        and (n // owners * owners * rows) % (16 * group) == 0
+        and n * rows * width * group * 12 < 40 * 1024 * 1024
+        and group > 1
+        and owners > 1
+    )
+    if fits:
+        return fused_step(mesh, grad_parts, momentum, layer_live)
+    return per_device(grad_parts, momentum, layer_live)
+
+
 def solution(mesh):
     placed = (P(("rep", "grp"), None, "dp", None), P(None, "dp", ("rep", "grp")), P())
     return jax.shard_map(
-        per_device,
+        functools.partial(per_device_step, mesh),
         mesh=mesh,
         in_specs=placed,
         out_specs=(P(None, "dp", ("rep", "grp")), P(None, "dp", ("rep", "grp"))),

time: 202 us -> 52.3 us (0.26)
  waiting for transfers between devices: 152 us -> 0 us
  Pallas kernels: 0 us -> 46.4 us
  starting transfers between devices: 13.6 us -> 0 us
  between operations: 14.1 us -> 0.64 us
  other arithmetic: 7.27 us -> 0.66 us
  local copies, waits for them, and re-layouts: 9.57 us -> 4.39 us
  matrix products: 4.55 us -> 0 us
    all_to_all x2 -> x0, waiting for transfers between devices: 73.6 us -> none  [the longest x1 37.4 us: per_device(): lax.all_to_all(outgoing, 'dp', split_axis=1, concat_axis=1, tiled=True)]
    reduce_scatter x1 -> x0, waiting for transfers between devices: 52.2 us -> none  [per_device(): lax.psum_scatter(grad_parts[0], ('rep', 'grp'), scatter_dimension=2, tile...]
    pallas_call x0 -> x1, Pallas kernels: none -> 46.4 us  [fused_step(): pl.pallas_call(functools.partial(step_kernel, (group, owners, per_group,...]
    all_gather x1 -> x0, waiting for transfers between devices: 25.8 us -> none  [per_device(): lax.all_gather(fresh_momentum.astype(jnp.bfloat16), ('rep', 'grp'), axis=...]
    all_to_all x2 -> x0, starting transfers between devices: 13.5 us -> none  [the longest x1 8.88 us: per_device(): lax.all_to_all(results, 'dp', split_axis=1, concat_axis=1, tiled=True)]
    dot_general x10 -> x0, matrix products: 4.55 us -> none  [the longest x5 2.59 us: newton_schulz(): jnp.dot(polynomial, current, preferred_element_type=jnp.float32)]
    unnamed x4 -> x6, local copies, waits for them, and re-layouts: 0.01 us -> 4.31 us
    reshape x1 -> x0, local copies, waits for them, and re-layouts: 2.74 us -> none  [per_device(): results = results.reshape(item_count, owners, piece_rows, col_count)]
  transfers between devices with their start and end apart: 4 -> 0, of which waited for: 4 -> 0; matrix products, arithmetic and copies ran while one was open for 0% -> 0% of each run, Pallas kernels for 0% -> 0%
where the time goes in v1:
time: 52.3 us; the launch traced here: 52.1 us
  Pallas kernels  46.4 us (89%)
  local copies, waits for them, and re-layouts  4.39 us (8%)
  other arithmetic  0.66 us (1%)
  between operations  0.64 us (1%)
    pallas_call x1, Pallas kernels, fused_step(): pl.pallas_call(functools.partial(step_kernel, (group, owners, per_group,...  46.4 us
    unnamed x6, local copies, waits for them, and re-layouts  4.31 us

profile of v1, /device:TPU:0, one launch (start us, length us, event | category | flops | bytes accessed | tf_op | source)
XLA Modules:
  0.0 52.1 jit_solution(11966709586398092090)
XLA Ops:
  0.6 0.7 %convert_element_type.3 = f32[8]{0:T(128)S(1)} convert(s32[8]{0:T(128)} %param.5) | non-fusion elementwise | flops 8 | bytes 64 | tf_op jit(solution)/shard_map/convert_element_type | solution.py:273
  1.3 0.1 broadcast_in_dim.2.live_ref
  1.4 0.0 copy-start
  1.4 1.9 %copy-done = f32[1,8,48,2048]{3,2,1,0:T(8,128)S(1)} copy-done((f32[1,8,48,2048]{3,2,1,0:T(8,128)S(1)}, f32[1,8,48,2048]{3,2,1,0:T(8,128)}, u32[]{:S(2)}) %copy-start) | copy-done | bytes 3145752
  3.3 0.0 copy-start.1
  3.3 1.0 %copy-done.1 = f32[8,48,256]{2,1,0:T(8,128)S(1)} copy-done((f32[8,48,256]{2,1,0:T(8,128)S(1)}, f32[8,48,256]{2,1,0:T(8,128)}, u32[]{:S(2)}) %copy-start.1) | copy-done | bytes 393240
  4.3 46.4 %shard_map.50 = (f32[8,48,256]{2,1,0:T(8,128)S(1)}, bf16[8,48,256]{2,1,0:T(8,128)(2,1)S(1)}) custom-call(f32[1,8,48,2048]{3,2,1,0:T(8,128)S(1)} %copy-done, f32[8,48,256]{2,1,0:T(8,128)S(1)} %copy-done.1, f32[8,1,256]{2,1,0:T(1,128)S(1)} %broadcast_in_dim.2.live_ref), custom_call_target="tpu_custom_call" | custom-call | tf_op jit(solution)/shard_map/pallas_call | solution.py:277
  50.7 0.7 %copy.7 = f32[8,48,256]{2,1,0:T(8,128)} copy(f32[8,48,256]{2,1,0:T(8,128)S(1)} %get-tuple-element.4) | data formatting | bytes 786432
  51.4 0.7 %copy.8 = bf16[8,48,256]{2,1,0:T(8,128)(2,1)} copy(bf16[8,48,256]{2,1,0:T(8,128)(2,1)S(1)} %get-tuple-element.5) | data formatting | bytes 393216
Async XLA Ops:
  1.4 1.9 %copy-start = (f32[1,8,48,2048]{3,2,1,0:T(8,128)S(1)}, f32[1,8,48,2048]{3,2,1,0:T(8,128)}, u32[]{:S(2)}) copy-start(f32[1,8,48,2048]{3,2,1,0:T(8,128)} %grad_ref.1) | copy-start | bytes 9437188
  3.3 1.0 %copy-start.1 = (f32[8,48,256]{2,1,0:T(8,128)S(1)}, f32[8,48,256]{2,1,0:T(8,128)}, u32[]{:S(2)}) copy-start(f32[8,48,256]{2,1,0:T(8,128)} %mom_ref.1) | copy-start | bytes 1179652
